TPU v7x, 512 devices: a whole 4x4x16 slice. The times are simulated.
512 devices in a mesh: pack: 16 (over y, x), seq: 32 (over z, core).
Axes of the slice: x: 4, y: 4, z: 16, core: 2. Of those that a mesh axis runs over, the one named last changes fastest.
Arguments:
- queries: bfloat16 [65536, 2048], P(('pack', 'seq')), parts along dimension 0, may hold values from -48 to 48
- token_key_heads: bfloat16 [65536, 256], P(('pack', 'seq')), parts along dimension 0, may hold values from -6 to 6
- token_value_heads: bfloat16 [65536, 256], P(('pack', 'seq')), parts along dimension 0, may hold values from -6 to 6
- residual: bfloat16 [65536, 1024], P(('pack', 'seq')), parts along dimension 0, may hold values from -40 to 40
- out_weight: bfloat16 [2048, 1024], P('seq'), may hold values from -0.125 to 0.125
- norm_gain: bfloat16 [1024], replicated, may hold values from 0.5 to 1.5
- w_gate: bfloat16 [32, 1024, 384], P('seq'), may hold values from -0.1875 to 0.1875
- w_up: bfloat16 [32, 1024, 384], P('seq'), may hold values from -0.1875 to 0.1875
- w_down: bfloat16 [32, 384, 1024], P('seq'), may hold values from -0.3125 to 0.3125
- expert_ids: int32 [65536, 8], P(('pack', 'seq')), parts along dimension 0, may hold values from 0 to 31, all different within a row; in each aligned block of 128 rows (0 to 127, 128 to 255, ...) at most 48 rows name the same one
- gate_weights: float32 [65536, 8], P(('pack', 'seq')), parts along dimension 0, may hold values from 0.05 to 0.3
- doc_of_block: int32 [512], P('pack'), parts along dimension 0, may hold values from 0 to 7, never falling along the last dimension, each value on 1 to 8 neighbouring positions
Outputs:
- attention: bfloat16 [65536, 2048], P(('pack', 'seq')), parts along dimension 0
- hidden_out: bfloat16 [65536, 1024], P(('pack', 'seq')), parts along dimension 0
- expert_mix: bfloat16 [65536, 1024], P(('pack', 'seq')), parts along dimension 0
There are 16 independent parts, one for each index of `pack`. A program takes and returns all parts, laid end to end along the dimension named above; an argument that names none is the same for every part. Nothing has to cross between parts.
Inputs may be any that keep to these rules, and one draw needn't show every extreme that they name: `expert_ids`: each row names 8 different experts; within the rows of one block no expert is named more than 48 times, and in every draw some expert is named exactly 48 times by the rows of some block. `doc_of_block`: never falls from block to block; each document covers 1 to 8 blocks, one exactly 8.
All inputs are finite; a program needn't handle non-finite values.
Results may differ from a plain program's by a relative error of at most 0.015.
Values may be sent and summed in bfloat16 or wider, within the bound.
A program may use at most 64 MiB of HBM per device.

v0:
```python
import math

import jax
import jax.numpy as jnp
from jax import lax
from jax.sharding import PartitionSpec as P

QUERY_HEADS = 16
KEY_VALUE_HEADS = 2
HEAD_SIZE = 128
TOP = 8


def attend(queries, key_token_rows, value_token_rows, query_pos, key_pos, allowed):
    token_rows = queries.shape[0]
    heads_per_group = QUERY_HEADS // KEY_VALUE_HEADS
    token_query_heads = queries.reshape(token_rows, KEY_VALUE_HEADS, heads_per_group, HEAD_SIZE)
    key_count = key_token_rows.shape[0]
    tile_length = math.gcd(key_count, 512)
    number_of_tiles = key_count // tile_length
    key_tile_list = key_token_rows.reshape(number_of_tiles, tile_length, KEY_VALUE_HEADS, HEAD_SIZE)
    value_tile_list = value_token_rows.reshape(
        number_of_tiles, tile_length, KEY_VALUE_HEADS, HEAD_SIZE
    )
    pos_tiles = key_pos.reshape(number_of_tiles, tile_length)
    allowed_tiles = allowed.reshape(number_of_tiles, tile_length)
    factor = 1.0 / HEAD_SIZE**0.5

    def tile_step(running, tile):
        key_tile, value_tile, pos_tile, allowed_tile = tile
        visible = allowed_tile[None, :] & (pos_tile[None, :] <= query_pos[:, None])

        def compute(current):
            run_max, run_sum, accum = current
            scores = (
                jnp.einsum(
                    "tkgd,skd->kgts",
                    token_query_heads,
                    key_tile,
                    preferred_element_type=jnp.float32,
                )
                * factor
            )
            scores = jnp.where(visible, scores, -1e30)
            new_max = jnp.maximum(run_max, jnp.max(scores, axis=-1))
            terms = jnp.where(visible, jnp.exp(scores - new_max[..., None]), 0.0)
            rescale = jnp.exp(run_max - new_max)
            new_sum = run_sum * rescale + jnp.sum(terms, axis=-1)
            product = jnp.einsum(
                "kgts,skd->kgtd",
                terms.astype(jnp.bfloat16),
                value_tile,
                preferred_element_type=jnp.float32,
            )
            return (new_max, new_sum, accum * rescale[..., None] + product)

        return (lax.cond(jnp.any(visible), compute, lambda current: current, running), None)

    start_state = (
        jnp.full((KEY_VALUE_HEADS, heads_per_group, token_rows), -1e30, jnp.float32),
        jnp.zeros((KEY_VALUE_HEADS, heads_per_group, token_rows), jnp.float32),
        jnp.zeros((KEY_VALUE_HEADS, heads_per_group, token_rows, HEAD_SIZE), jnp.float32),
    )
    final_state, _ = lax.scan(
        tile_step, start_state, (key_tile_list, value_tile_list, pos_tiles, allowed_tiles)
    )
    run_max, run_sum, accum = final_state
    result = accum / run_sum[..., None]
    return (
        jnp.transpose(result, (2, 0, 1, 3))
        .reshape(token_rows, QUERY_HEADS * HEAD_SIZE)
        .astype(jnp.bfloat16)
    )


def expert_rows(arrived, gate_proj, up_proj, down_proj):
    sources, slot_count, width = arrived.shape
    flat_rows = arrived.reshape(sources * slot_count, width)
    gate_part = jnp.dot(flat_rows, gate_proj, preferred_element_type=jnp.float32)
    up_part = jnp.dot(flat_rows, up_proj, preferred_element_type=jnp.float32)
    activated = (jax.nn.silu(gate_part) * up_part).astype(jnp.bfloat16)
    produced = jnp.dot(activated, down_proj, preferred_element_type=jnp.float32).astype(
        jnp.bfloat16
    )
    return produced.reshape(sources, slot_count, width)


def shards(
    queries,
    token_key_heads,
    token_value_heads,
    residual,
    out_weight,
    norm_gain,
    w_gate,
    w_up,
    w_down,
    expert_ids,
    gate_weights,
    doc_of_block,
):
    token_rows = queries.shape[0]
    blocks = lax.axis_size("seq")
    own_index = lax.axis_index("seq")
    local_pos = jnp.arange(token_rows, dtype=jnp.int32)
    query_pos = own_index * token_rows + local_pos
    own_doc = doc_of_block[own_index]
    key_head_width = token_key_heads.shape[1]
    key_token_rows, value_token_rows = (
        lax.all_gather(token_key_heads, "seq", axis=0, tiled=True),
        lax.all_gather(token_value_heads, "seq", axis=0, tiled=True),
    )
    key_pos = jnp.arange(blocks * token_rows, dtype=jnp.int32)
    key_block = key_pos // token_rows
    allowed = (key_block <= own_index) & ((doc_of_block[key_block] == own_doc) | (key_block == 0))
    key_token_rows = key_token_rows.reshape(
        key_token_rows.shape[0], KEY_VALUE_HEADS, key_head_width // KEY_VALUE_HEADS
    )
    value_token_rows = value_token_rows.reshape(
        value_token_rows.shape[0], KEY_VALUE_HEADS, key_head_width // KEY_VALUE_HEADS
    )
    attention = attend(queries, key_token_rows, value_token_rows, query_pos, key_pos, allowed)
    width = residual.shape[1]
    projected = jnp.dot(
        attention,
        lax.all_gather(out_weight, "seq", axis=0, tiled=True),
        preferred_element_type=jnp.float32,
    )
    hidden_state = residual.astype(jnp.float32) + projected
    mean_square = jnp.mean(hidden_state * hidden_state, axis=-1, keepdims=True)
    normed = (hidden_state * lax.rsqrt(mean_square + 1e-06) * norm_gain.astype(jnp.float32)).astype(
        jnp.bfloat16
    )
    slot_cap = min(token_rows, 3 * token_rows * TOP // (2 * blocks))
    routed_ids = expert_ids.reshape(-1)
    one_hot = (routed_ids[:, None] == jnp.arange(blocks, dtype=jnp.int32)[None, :]).astype(
        jnp.int32
    )
    earlier = jnp.cumsum(one_hot, axis=0) - one_hot
    slot_pos = jnp.sum(earlier * one_hot, axis=1)
    slot_index = routed_ids * slot_cap + slot_pos
    token_of = jnp.arange(token_rows * TOP, dtype=jnp.int32) // TOP
    outgoing = (
        jnp.zeros((blocks * slot_cap, width), jnp.bfloat16).at[slot_index].set(normed[token_of])
    )
    outgoing = outgoing.reshape(blocks, slot_cap, width)
    arrived = lax.all_to_all(outgoing, "seq", split_axis=0, concat_axis=0, tiled=True)
    served = expert_rows(arrived, w_gate[0], w_up[0], w_down[0])
    returned_rows = lax.all_to_all(served, "seq", split_axis=0, concat_axis=0, tiled=True)
    picked = returned_rows.reshape(blocks * slot_cap, width)[slot_index].astype(jnp.float32)
    weighted = picked * gate_weights.reshape(-1)[:, None]
    expert_mix = jnp.sum(weighted.reshape(token_rows, TOP, width), axis=1).astype(jnp.bfloat16)
    return (attention, hidden_state.astype(jnp.bfloat16), expert_mix)


def solution(mesh):
    in_specs = (
        P(("pack", "seq"), None),
        P(("pack", "seq"), None),
        P(("pack", "seq"), None),
        P(("pack", "seq"), None),
        P("seq", None),
        P(),
        P("seq", None, None),
        P("seq", None, None),
        P("seq", None, None),
        P(("pack", "seq"), None),
        P(("pack", "seq"), None),
        P("pack"),
    )
    out_specs = (P(("pack", "seq"), None), P(("pack", "seq"), None), P(("pack", "seq"), None))
    return jax.shard_map(shards, mesh=mesh, in_specs=in_specs, out_specs=out_specs, check_vma=False)
```

profile of v0, /device:TPU:1, one launch (start us, length us, event | category | flops | bytes accessed | tf_op | source)
XLA Modules:
  0.0 579.3 jit_solution(16247242193508925619)
XLA Ops:
  11.9 1.9 fusion.43
  13.8 2.1 fusion.42
  15.8 4.5 compare_select_fusion.1
  20.3 16.1 %select_compare_fusion = pred[4096]{0:T(1024)(128)(4,1)S(1)} fusion(pred[4096]{0:T(1024)(128)(4,1)S(1)} %compare_reduce_fusion, pred[4096]{0:T(1024)(128)(4,1)S(1)} %compare_reduce_fusion.1, pred[4096]{0:T(1024)(128)(4,1)S(1)} %compare_reduce_fusion.2, pred[4096]{0:T(1024)(128)(4,1)S(1)} %compare_reduce_fusion.3, ...), kind=kLoop, calls=%fused_computation.99 | loop fusion | flops 106496 | bytes 122984 | tf_op jit(solution)/shard_map/eq | solution.py:115
  38.7 9.0 %reduce-window.6 = s32[32,8,128]{2,1,0:T(8,128)S(1)} reduce-window(s32[32,8,128]{2,1,0:T(8,128)S(1)} %fusion.37, s32[]{:T(128)} %copy.62), window={size=1x1x128 pad=0_0x0_0x127_0}, to_apply=%region_7.8 | reduce-window | flops 4161536 | bytes 262148 | tf_op jit(solution)/shard_map/reduce-window
  48.6 39.2 %all-gather.4.cloned.1.call-done = bf16[4096,256]{1,0:T(8,128)(2,1)} async-done(((bf16[128,256]{1,0:T(8,128)(2,1)}), bf16[4096,256]{1,0:T(8,128)(2,1)}) %all-gather.4.cloned.1.call-update) | async-done | bytes 2097168 | tf_op jit(solution)/shard_map/all_gather | solution.py:110
  87.7 2.5 reshape.356
  90.3 1.8 copy.22
  92.1 66.5 %all-gather.6.cloned.1.call-done = bf16[4096,256]{1,0:T(8,128)(2,1)} async-done(((bf16[128,256]{1,0:T(8,128)(2,1)}), bf16[4096,256]{1,0:T(8,128)(2,1)}) %all-gather.6.cloned.1.call-update) | async-done | bytes 2097168 | tf_op jit(solution)/shard_map/all_gather | solution.py:111
  158.6 2.5 reshape.357
  161.2 1.8 copy.24
  163.0 18.0 %while.15 = (s32[]{:T(128)}, f32[2,8,128]{2,1,0:T(8,128)S(1)}, f32[2,8,128]{2,1,0:T(8,128)S(1)}, f32[2,8,128,128]{3,2,1,0:T(8,128)S(1)}, pred[8,512]{1,0:T(8,128...) while((s32[]{:T(128)}, f32[2,8,128]{2,1,0:T(8,128)S(1)}, ...), condition=%wide.region_6.7_spmd.clone, body=%wide.region_0.6_spmd.clone.sunk | while | flops 551227520 | bytes 16131831 | solution.py:64
  164.6 5.4 conditional.3
  167.3 2.6 fusion.8
  181.9 49.5 %all-gather.8.cloned.1.call-done = bf16[2048,1024]{1,0:T(8,128)(2,1)} async-done(((bf16[64,1024]{1,0:T(8,128)(2,1)}), bf16[2048,1024]{1,0:T(8,128)(2,1)}) %all-gather.8.cloned.1.call-update) | async-done | bytes 4194320 | tf_op jit(solution)/shard_map/all_gather | solution.py:126
  231.4 3.0 multiply_reduce_fusion
  235.2 14.9 %scatter_custom_fusion = bf16[1536,1024]{1,0:T(8,128)(2,1)} fusion(s32[1024]{0:T(1024)S(1)} %bitcast.128, bf16[128,1024]{1,0:T(8,128)(2,1)S(1)} %get-tuple-element.196, s32[1024]{0:T(1024)S(1)} %broadcast_clamp_fusion.1, bf16[]{:T(256)} %constant.107.clone.1), kind=kCustom, calls=%fused_computation.34 | custom fusion | bytes 3145730 | tf_op jit(solution)/shard_map/scatter | solution.py:144
  250.1 154.1 %all_to_all.10 = bf16[32,48,1024]{2,1,0:T(8,128)(2,1)S(1)} all-to-all(bf16[32,48,1024]{2,1,0:T(8,128)(2,1)} %bitcast.115), channel_id=1, replica_groups=mesh['pack'=16,'seq'=32] {'seq'}, dimensions={0} | all-to-all | bytes 6291456 | tf_op jit(solution)/shard_map/all_to_all | solution.py:147
  405.9 3.3 fusion.31
  409.2 7.8 %convolution_convert_fusion = bf16[1536,1024]{1,0:T(8,128)(2,1)} fusion(bf16[1536,1024]{1,0:T(8,128)(2,1)} %bitcast.118, f32[1536,384]{1,0:T(8,128)} %fusion.31, bf16[1,384,1024]{2,1,0:T(8,128)(2,1)S(1)} %copy-done, bf16[1,1024,384]{2,1,0:T(8,128)(2,1)S(1)} %copy-done.7), kind=kOutput, calls=%fused_computation.31 | convolution fusion | flops 2421030912 | bytes 10223616 | tf_op jit(solution)/shard_map/dot_general | solution.py:82
  417.0 5.0 all-to-all-start.1
  422.1 141.4 %all-to-all-done.1 = bf16[32,48,1024]{2,1,0:T(8,128)(2,1)} async-done(((bf16[32,48,1024]{2,1,0:T(8,128)(2,1)}), bf16[32,48,1024]{2,1,0:T(8,128)(2,1)}, u32[]{:S(2)}, u32[]{:S(2)}) %all-to-all-start.1) | async-done | bytes 3145760 | tf_op jit(solution)/shard_map/all_to_all | solution.py:149
  563.5 7.3 %gather_fusion = bf16[1024,1024]{1,0:T(8,128)(2,1)S(1)} fusion(bf16[1536,1024]{1,0:T(8,128)(2,1)} %bitcast.54, s32[1024]{0:T(1024)S(1)} %broadcast_clamp_fusion), kind=kCustom, calls=%fused_computation.1 | custom fusion | bytes 4198400 | tf_op jit(solution)/shard_map/gather | solution.py:150
  570.8 2.0 fusion.22
  (124 shorter events, 21.0 us)
Async XLA Ops:
  7.2 402.0 %copy-start = (bf16[1,384,1024]{2,1,0:T(8,128)(2,1)S(1)}, bf16[1,384,1024]{2,1,0:T(8,128)(2,1)}, u32[]{:S(2)}) copy-start(bf16[1,384,1024]{2,1,0:T(8,128)(2,1)} %param.24) | copy-start | bytes 2359300
  7.2 40.9 %copy-start.4 = (s32[128,8]{0,1:T(8,128)S(1)}, s32[128,8]{0,1:T(8,128)}, u32[]{:S(2)}) copy-start(s32[128,8]{0,1:T(8,128)} %param.25) | copy-start | bytes 12292
  7.2 80.5 %all-gather.4.cloned.1.call-start = ((), (), s32[]{:S(2)}) async-start(), calls=%async_computation.2 | async-start | bytes 2162688 | tf_op jit(solution)/shard_map/all_gather | solution.py:110
  7.9 150.7 %all-gather.6.cloned.1.call-start = ((), (), s32[]{:S(2)}) async-start(), calls=%async_computation.3 | async-start | bytes 2162688 | tf_op jit(solution)/shard_map/all_gather | solution.py:111
  8.7 222.7 %all-gather.8.cloned.1.call-start = ((), (), s32[]{:S(2)}) async-start(), calls=%async_computation.4 | async-start | bytes 4325376 | tf_op jit(solution)/shard_map/all_gather | solution.py:126
  181.1 50.3 %copy-start.3 = (bf16[128,1024]{1,0:T(8,128)(2,1)S(1)}, bf16[128,1024]{1,0:T(8,128)(2,1)}, u32[]{:S(2)}) copy-start(bf16[128,1024]{1,0:T(8,128)(2,1)} %param.19) | copy-start | bytes 786436
  181.9 53.3 %copy-start.2 = (bf16[16,8,16,128]{3,1,2,0:T(8,128)(2,1)}, bf16[16,8,16,128]{3,1,2,0:T(8,128)(2,1)S(1)}, u32[]{:S(2)}) copy-start(bf16[16,8,16,128]{3,1,2,0:T(8,128)(2,1)S(1)} %copy.43) | copy-start | bytes 1572868
  250.1 155.8 %copy-start.6 = (bf16[1,1024,384]{2,1,0:T(8,128)(2,1)S(1)}, bf16[1,1024,384]{2,1,0:T(8,128)(2,1)}, u32[]{:S(2)}) copy-start(bf16[1,1024,384]{2,1,0:T(8,128)(2,1)} %param.22) | copy-start | bytes 2359300
  404.2 1.7 copy-start.1
  405.9 3.3 copy-start.7
  417.0 5.0 copy-start.5
  417.0 146.5 %all-to-all-start.1 = ((bf16[32,48,1024]{2,1,0:T(8,128)(2,1)}), bf16[32,48,1024]{2,1,0:T(8,128)(2,1)}, u32[]{:S(2)}, u32[]{:S(2)}) async-start(bf16[32,48,1024]{2,1,0:T(8,128)(2,1)} %bitcast.116), calls=%async_computation.1 | async-start | bytes 6291456 | tf_op jit(solution)/shard_map/all_to_all | solution.py:149
Sparse Core Ops, SparseCore 0:
  10.1 77.5 all-gather.3
  89.9 68.6 all-gather.5
  160.7 70.6 all-gather.7
where the time goes:
time: 584 us; the launch traced here: 579 us
  waiting for transfers between devices  299 us (51%)
  blocking collectives  154 us (26%)
  other arithmetic  42.8 us (7%)
  local copies, waits for them, and re-layouts  40.6 us (7%)
  matrix products  18.4 us (3%)
  between operations  14 us (2%)
    all_to_all x1, blocking collectives, shards(): lax.all_to_all(outgoing, 'seq', split_axis=0, concat_axis=0, tiled=True)  154 us
    all_to_all x1, waiting for transfers between devices, shards(): lax.all_to_all(served, 'seq', split_axis=0, concat_axis=0, tiled=True)  141 us
    all_gather x1, waiting for transfers between devices, shards(): lax.all_gather(token_value_heads, 'seq', axis=0, tiled=True)  66.5 us
    all_gather x1, waiting for transfers between devices, shards(): lax.all_gather(out_weight, 'seq', axis=0, tiled=True)  49.5 us
    all_gather x1, waiting for transfers between devices, shards(): lax.all_gather(token_key_heads, 'seq', axis=0, tiled=True)  39.2 us
    eq x1, other arithmetic, shards(): doc_of_block[key_block] == own_doc  16.1 us
    scatter x1, local copies, waits for them, and re-layouts, shards(): jnp.zeros((blocks * slot_cap, width), jnp.bfloat16).at[slot_index]  14.9 us
  transfers between devices with their start and end apart: 4, of which 4 were waited for; matrix products, arithmetic and copies ran while one was open for 11% of the time, Pallas kernels for 0%

commit v1 on v0

v1 whole, which is shorter than its diff:
```python
import functools

import jax
import jax.numpy as jnp
from jax import lax
from jax.experimental import pallas as pl
from jax.experimental.pallas import tpu as pltpu
from jax.sharding import PartitionSpec as P

QUERY_HEADS = 16
KEY_VALUE_HEADS = 2
HEAD_SIZE = 128
TOP = 8
MESH = pl.DeviceIdType.MESH
HIDE = -1e30


def slab_kernel(
    chips,
    window,
    doc_ref,
    q_ref,
    k_ref,
    v_ref,
    res_ref,
    wo_ref,
    gain_ref,
    ids_ref,
    gw_ref,
    wg_hbm,
    wu_hbm,
    wd_hbm,
    attn_out,
    hid_out,
    mix_out,
    kv,
    qs,
    run_max,
    run_sum,
    oacc,
    heads,
    wfull,
    hidden,
    gate_send,
    gates,
    gate_cols,
    wgu,
    wd,
    xbuf,
    accbuf,
    contrib,
    own_part,
    kv_s,
    kv_r,
    sib_s,
    sib_r,
    first_s,
    first_r,
    w_s,
    w_r,
    wsib_s,
    wsib_r,
    g_s,
    g_r,
    load_s,
    ew_s,
    ew_r,
    x_s,
    x_r,
    a_s,
    a_r,
):
    me = lax.axis_index("seq")
    chip, core = me // 2, me % 2
    sib = chip * 2 + (1 - core)
    group = QUERY_HEADS // KEY_VALUE_HEADS
    tokens, width = res_ref.shape
    half = tokens // 2
    kvw = k_ref.shape[1]
    ff = wg_hbm.shape[2]
    hops = window // 2
    relay, first = window, window + 1

    def wrap(c):
        return lax.rem(c + 4 * chips, chips)

    def at(c):
        return wrap(c) * 2 + core

    nxt, prv = at(chip + 1), at(chip - 1)

    def rcopy(src, dst, ssem, rsem, dev):
        return pltpu.make_async_remote_copy(
            src_ref=src,
            dst_ref=dst,
            send_sem=ssem,
            recv_sem=rsem,
            device_id={"seq": dev},
            device_id_type=MESH,
        )

    def kv_hop(t):
        return rcopy(kv.at[2 * t], kv.at[2 * t + 2], kv_s.at[t], kv_r.at[t], nxt)

    def kv_share(t):
        return rcopy(
            kv.at[2 * t], kv.at[2 * (t - core) + 1], sib_s.at[t - core], sib_r.at[t - core], sib
        )

    def kv_shared(t):
        return rcopy(kv.at[2 * t + 1], kv.at[2 * t + 1], sib_s.at[t], sib_r.at[t], sib)

    def w_chip(d, t):
        return wrap(chip - t) if d == 0 else wrap(chip + t)

    def w_hop(d, t):
        ref = wfull.at[w_chip(d, t) * 2 + core]
        return rcopy(ref, ref, w_s.at[d, t], w_r.at[d, t], nxt if d == 0 else prv)

    def w_arrived(d, t):
        ref = wfull.at[w_chip(d, t) * 2 + core]
        return rcopy(ref, ref, w_s.at[d, t - 1], w_r.at[d, t - 1], nxt if d == 0 else prv)

    def w_share(d, t):
        ref = wfull.at[w_chip(d, t) * 2 + core]
        return rcopy(ref, ref, wsib_s.at[d, t], wsib_r.at[d, t], sib)

    def w_shared(d, t):
        ref = wfull.at[w_chip(d, t) * 2 + (1 - core)]
        return rcopy(ref, ref, wsib_s.at[d, t], wsib_r.at[d, t], sib)

    def gate_copy(d):
        to = wrap(chip + d)
        return rcopy(gate_send.at[to], gates.at[chip], g_s.at[d], g_r.at[d], to * 2 + core)

    def gate_arrived(d):
        ref = gates.at[wrap(chip - d)]
        return rcopy(ref, ref, g_s.at[d], g_r.at[d], nxt)

    def first_copy(n, dev):
        return rcopy(kv.at[first], kv.at[first], first_s.at[n], first_r, dev)

    def cols(e):
        return pl.ds(pl.multiple_of(e * ff, 128), ff)

    def up_cols(e):
        return pl.ds(pl.multiple_of((2 + e) * ff, 128), ff)

    def rows(e):
        return pl.ds(pl.multiple_of(e * ff, 128), ff)

    weights = (
        (wg_hbm.at[0], wgu.at[:, cols(core)], wgu.at[:, cols(1 - core)]),
        (wu_hbm.at[0], wgu.at[:, up_cols(core)], wgu.at[:, up_cols(1 - core)]),
        (wd_hbm.at[0], wd.at[rows(core)], wd.at[rows(1 - core)]),
    )

    def x_hop(d, s):
        return rcopy(
            xbuf.at[d, s], xbuf.at[d, s + 1], x_s.at[d, s], x_r.at[d, s], nxt if d == 0 else prv
        )

    def a_hop(d, s):
        return rcopy(
            accbuf.at[d, s], accbuf.at[d, s + 1], a_s.at[d, s], a_r.at[d, s], nxt if d == 0 else prv
        )

    kv[0, :, :kvw] = k_ref[...]
    kv[0, :, kvw:] = v_ref[...]
    wfull[me] = wo_ref[...]
    barrier = pltpu.get_barrier_semaphore()

    def greet(d, carry):
        pl.semaphore_signal(
            barrier, inc=1, device_id={"seq": at(chip + d)}, device_id_type=MESH
        )
        return carry

    lax.fori_loop(1, chips, greet, 0)
    pl.semaphore_signal(barrier, inc=1, device_id={"seq": sib}, device_id_type=MESH)
    pl.semaphore_wait(barrier, chips)

    kv_hop(0).start()

    @pl.when(core == 0)
    def _():
        kv_share(0).start()

    w_hop(1, 0).start()

    reached = tuple(range(chips - 1, 4, -2))

    @pl.when(me == 0)
    def _():
        for n, c in enumerate(reached):
            rcopy(kv.at[0], kv.at[first], first_s.at[n], first_r, 2 * c).start()

    w_hop(0, 0).start()
    w_share(0, 0).start()

    @pl.when(chip < 4)
    def _():
        kv[first] = kv[0]

    for n, (src, mine, _) in enumerate(weights):
        pltpu.make_async_copy(src, mine, load_s.at[n]).start()

    lane = lax.broadcasted_iota(jnp.int32, (tokens, 128), 1)
    dense = jnp.zeros((tokens, 128), jnp.float32)
    for n in range(TOP):
        dense = dense + jnp.where(lane == ids_ref[:, n : n + 1], gw_ref[:, n : n + 1], 0.0)
    by_expert = dense.T
    for c in range(chips):
        gate_send[c] = by_expert[2 * c : 2 * c + 2]
    gates[chip] = gate_send[chip]

    def send_gates(d, carry):
        gate_copy(d).start()
        return carry

    lax.fori_loop(1, chips, send_gates, 0)

    for h in range(QUERY_HEADS):
        qs[h // group, (h % group) * tokens : (h % group + 1) * tokens, :] = q_ref[
            :, h * HEAD_SIZE : (h + 1) * HEAD_SIZE
        ]
    run_max[...] = jnp.full_like(run_max, HIDE)
    run_sum[...] = jnp.zeros_like(run_sum)
    oacc[...] = jnp.zeros_like(oacc)
    factor = 1.0 / HEAD_SIZE**0.5

    def attend(slot, seen):
        key_at = lax.broadcasted_iota(jnp.int32, (tokens, tokens), 0)
        query_at = lax.broadcasted_iota(jnp.int32, (tokens, tokens), 1)
        bias = jnp.where(seen, 0.0, HIDE).astype(jnp.float32)
        late = (key_at > query_at) & (slot == 0)
        tile = jnp.where(late, HIDE, bias)
        tile = jnp.concatenate([tile] * group, axis=1)
        for g in range(KEY_VALUE_HEADS):
            keys = kv[slot, :, g * HEAD_SIZE : (g + 1) * HEAD_SIZE]
            values = kv[slot, :, kvw + g * HEAD_SIZE : kvw + (g + 1) * HEAD_SIZE]
            s = lax.dot_general(
                keys, qs[g], (((1,), (1,)), ((), ())), preferred_element_type=jnp.float32
            )
            s = s * factor + tile
            old = run_max[g]
            new = jnp.maximum(old, jnp.max(s, axis=0, keepdims=True))
            p = jnp.exp(s - new)
            fade = jnp.exp(old - new)
            run_max[g] = new
            run_sum[g] = run_sum[g] * fade + jnp.sum(p, axis=0, keepdims=True)
            oacc[g] = oacc[g] * fade + lax.dot_general(
                values,
                p.astype(jnp.bfloat16),
                (((0,), (0,)), ((), ())),
                preferred_element_type=jnp.float32,
            )

    own_doc = doc_ref[me]

    def seen_of(slot):
        blk = me - slot
        doc = doc_ref[jnp.maximum(blk, 0)]
        return (blk == 0) | ((blk > 0) & (doc == own_doc))

    def w_step(t, down=True):
        if down:
            w_arrived(0, t).wait_recv()

            @pl.when(t < chips // 2 - 1)
            def _():
                w_hop(0, t).start()

            w_share(0, t).start()
        w_arrived(1, t).wait_recv()

        @pl.when(t < chips // 2)
        def _():
            w_hop(1, t).start()

        w_share(1, t).start()

    for n, (src, mine, _) in enumerate(weights):
        pltpu.make_async_copy(src, mine, load_s.at[n]).wait()
        rcopy(mine, mine, ew_s.at[n], ew_r.at[n], sib).start()

    attend(0, me >= 0)

    def window_step(t, carry):
        kv_hop(t - 1).wait_recv()

        @pl.when((t < hops - 1) | (core == 1))
        def _():
            kv_hop(t).start()

        kv_share(t).start()
        w_step(t)

        def both(n, inner):
            slot = 2 * t - n

            @pl.when(n == 1)
            def _():
                kv_shared(t - 1).wait_recv()

            attend(slot, seen_of(slot))
            return inner

        lax.fori_loop(0, 2, both, 0)

        @pl.when((t == 2) & (core == 0) & (chip >= 5) & (chip % 2 == 1))
        def _():
            first_copy(0, sib).wait_recv()
            first_copy(0, at(chip - 1)).start()
            first_copy(1, sib).start()

        @pl.when((t == 3) & (core == 0) & (chip >= 4) & (chip % 2 == 0))
        def _():
            first_copy(1, sib).wait_recv()
            first_copy(1, sib).start()

        return carry

    lax.fori_loop(1, hops, window_step, 0)

    @pl.when(core == 1)
    def _():
        kv_hop(hops - 1).wait_recv()
        kv_share(hops).start()

    w_step(hops)
    kv_shared(hops - 1).wait_recv()

    @pl.when((core == 1) & (chip >= 4))
    def _():
        first_copy(0, sib).wait_recv()

    def rest(n, carry):
        slot = window - 1 + 2 * n
        attend(slot, ((n == 0) & seen_of(window - 1)) | ((n == 1) & (me >= window)))
        return carry

    lax.fori_loop(0, 2, rest, 0)

    for g in range(KEY_VALUE_HEADS):
        done = oacc[g] / run_sum[g]
        for n in range(group):
            h = g * group + n
            one = done[:, n * tokens : (n + 1) * tokens].T.astype(jnp.bfloat16)
            attn_out[:, h * HEAD_SIZE : (h + 1) * HEAD_SIZE] = one
            heads[h] = one

    hidden[...] = res_ref[...].astype(jnp.float32)

    def project(c):
        part = wfull[pl.ds(2 * c, 2)].reshape(2 * wo_ref.shape[0], width)
        hidden[...] += jnp.dot(heads[c], part, preferred_element_type=jnp.float32)

    w_shared(0, 0).wait_recv()
    project(chip)

    def project_step(t, carry):
        @pl.when(t > hops)
        def _():
            w_step(t)

        w_shared(0, t).wait_recv()
        project(w_chip(0, t))
        w_shared(1, t).wait_recv()
        project(w_chip(1, t))
        return carry

    lax.fori_loop(1, chips // 2, project_step, 0)
    w_step(chips // 2, down=False)
    w_shared(1, chips // 2).wait_recv()
    project(w_chip(1, chips // 2))

    state = hidden[...]
    hid_out[...] = state.astype(jnp.bfloat16)
    mean_square = jnp.mean(state * state, axis=-1, keepdims=True)
    normed = (
        state * lax.rsqrt(mean_square + 1e-06) * gain_ref[...].astype(jnp.float32)
    ).astype(jnp.bfloat16)
    xbuf[0, 0] = normed[:half]
    xbuf[1, 0] = normed[half:]
    for d in range(2):
        x_hop(d, 0).start()

    def wait_gates(d, carry):
        gate_arrived(d).wait_recv()
        return carry

    lax.fori_loop(1, chips, wait_gates, 0)
    stacked = jnp.concatenate(
        [gates[c] for c in range(chips)]
        + [jnp.zeros((128 - 2 * chips, tokens), jnp.float32)],
        axis=0,
    )
    gate_cols[...] = stacked.T
    for n, (_, _, theirs) in enumerate(weights):
        rcopy(theirs, theirs, ew_s.at[n], ew_r.at[n], sib).wait_recv()

    def served(s):
        row = lax.broadcasted_iota(jnp.int32, (tokens, 128), 0)
        x = xbuf[:, s].reshape(tokens, width)
        both = jnp.dot(x, wgu[...], preferred_element_type=jnp.float32)
        home = jnp.where(row < half, wrap(chip - s), wrap(chip + s)) * 2
        parts = []
        for e in range(2):
            gate = jnp.sum(
                jnp.where(lane == home + e, gate_cols[...], 0.0), axis=1, keepdims=True
            )
            v = both[:, e * ff : (e + 1) * ff]
            u = both[:, (2 + e) * ff : (3 + e) * ff]
            parts.append((v / (1.0 + jnp.exp(-v)) * u * gate).astype(jnp.bfloat16))
        return jnp.dot(
            jnp.concatenate(parts, axis=1), wd[...], preferred_element_type=jnp.float32
        )

    own_part[...] = served(0)
    last = chips - 1

    def take_x(s):
        for d in range(2):
            x_hop(d, s - 1).wait_recv()

            @pl.when(s < last)
            def _():
                x_hop(d, s).start()

    take_x(1)
    contrib[...] = served(1)

    def ring_step(s, carry):
        @pl.when(s < last)
        def _():
            take_x(s + 1)

        @pl.when(s > 1)
        def _():
            for d in range(2):
                a_hop(d, s - 1).wait_recv()
                part = slice(d * half, (d + 1) * half)
                accbuf[d, s] = (contrib[part] + accbuf[d, s].astype(jnp.float32)).astype(
                    jnp.bfloat16
                )
                a_hop(d, s).start()

        @pl.when(s == 1)
        def _():
            for d in range(2):
                accbuf[d, s] = contrib[d * half : (d + 1) * half].astype(jnp.bfloat16)
                a_hop(d, s).start()

        @pl.when(s < last)
        def _():
            contrib[...] = served(s + 1)

        return carry

    lax.fori_loop(1, chips, ring_step, 0)
    for d in range(2):
        a_hop(d, last).wait_recv()
        part = slice(d * half, (d + 1) * half)
        mix_out[part] = (own_part[part] + accbuf[d, chips].astype(jnp.float32)).astype(
            jnp.bfloat16
        )

    for t in range(hops - 1):
        kv_hop(t).wait_send()

    @pl.when(core == 1)
    def _():
        kv_hop(hops - 1).wait_send()

    for t in range(hops):
        kv_shared(t).wait_send()

    @pl.when(me == 0)
    def _():
        for n in range(len(reached)):
            first_copy(n, sib).wait_send()

    @pl.when((core == 0) & (chip >= 4))
    def _():
        first_copy(1, sib).wait_send()

    @pl.when((core == 0) & (chip >= 5) & (chip % 2 == 1))
    def _():
        first_copy(0, sib).wait_send()

    def sent_w(t, carry):
        w_hop(0, t).wait_send()
        w_hop(1, t).wait_send()
        w_share(0, t).wait_send()
        w_share(1, t + 1).wait_send()
        return carry

    lax.fori_loop(0, chips // 2 - 1, sent_w, 0)
    w_hop(1, chips // 2 - 1).wait_send()
    w_share(0, chips // 2 - 1).wait_send()
    w_share(1, chips // 2).wait_send()

    def sent(s, carry):
        gate_copy(s).wait_send()
        for d in range(2):
            x_hop(d, s - 1).wait_send()
            a_hop(d, s).wait_send()
        return carry

    lax.fori_loop(1, chips, sent, 0)
    for n, (_, mine, _) in enumerate(weights):
        rcopy(mine, mine, ew_s.at[n], ew_r.at[n], sib).wait_send()


def shards(
    queries,
    token_key_heads,
    token_value_heads,
    residual,
    out_weight,
    norm_gain,
    w_gate,
    w_up,
    w_down,
    expert_ids,
    gate_weights,
    doc_of_block,
):
    blocks = lax.axis_size("seq")
    chips = blocks // 2
    tokens, width = residual.shape
    heads_width = queries.shape[1]
    kvw = token_key_heads.shape[1]
    ff = w_gate.shape[2]
    window = 8
    group_rows = tokens * QUERY_HEADS // KEY_VALUE_HEADS
    half = tokens // 2
    vmem = pl.BlockSpec(memory_space=pltpu.VMEM)
    hbm = pl.BlockSpec(memory_space=pl.ANY)
    dma = pltpu.SemaphoreType.DMA
    bf16, f32 = jnp.bfloat16, jnp.float32
    return pl.pallas_call(
        functools.partial(slab_kernel, chips, window),
        out_shape=(
            jax.ShapeDtypeStruct((tokens, heads_width), bf16),
            jax.ShapeDtypeStruct((tokens, width), bf16),
            jax.ShapeDtypeStruct((tokens, width), bf16),
        ),
        in_specs=[pl.BlockSpec(memory_space=pltpu.SMEM)] + [vmem] * 8 + [hbm] * 3,
        out_specs=(vmem, vmem, vmem),
        scratch_shapes=[
            pltpu.VMEM((window + 2, tokens, 2 * kvw), bf16),
            pltpu.VMEM((KEY_VALUE_HEADS, group_rows, HEAD_SIZE), bf16),
            pltpu.VMEM((KEY_VALUE_HEADS, 1, group_rows), f32),
            pltpu.VMEM((KEY_VALUE_HEADS, 1, group_rows), f32),
            pltpu.VMEM((KEY_VALUE_HEADS, HEAD_SIZE, group_rows), f32),
            pltpu.VMEM((QUERY_HEADS, tokens, HEAD_SIZE), bf16),
            pltpu.VMEM((blocks, out_weight.shape[0], width), bf16),
            pltpu.VMEM((tokens, width), f32),
            pltpu.VMEM((chips, 2, tokens), f32),
            pltpu.VMEM((chips, 2, tokens), f32),
            pltpu.VMEM((tokens, 128), f32),
            pltpu.VMEM((width, 4 * ff), bf16),
            pltpu.VMEM((2 * ff, width), bf16),
            pltpu.VMEM((2, chips, half, width), bf16),
            pltpu.VMEM((2, chips + 1, half, width), bf16),
            pltpu.VMEM((tokens, width), f32),
            pltpu.VMEM((tokens, width), f32),
            dma((window // 2,)),
            dma((window // 2,)),
            dma((window // 2,)),
            dma((window // 2,)),
            dma((8,)),
            dma,
            dma((2, chips // 2)),
            dma((2, chips // 2)),
            dma((2, chips // 2 + 1)),
            dma((2, chips // 2 + 1)),
            dma((chips,)),
            dma((chips,)),
            dma((3,)),
            dma((3,)),
            dma((3,)),
            dma((2, chips)),
            dma((2, chips)),
            dma((2, chips)),
            dma((2, chips)),
        ],
        compiler_params=pltpu.CompilerParams(
            collective_id=0, has_side_effects=True, vmem_limit_bytes=48 << 20
        ),
    )(
        doc_of_block,
        queries,
        token_key_heads,
        token_value_heads,
        residual,
        out_weight,
        norm_gain.reshape(1, width),
        expert_ids,
        gate_weights,
        w_gate,
        w_up,
        w_down,
    )


def solution(mesh):
    in_specs = (
        P(("pack", "seq"), None),
        P(("pack", "seq"), None),
        P(("pack", "seq"), None),
        P(("pack", "seq"), None),
        P("seq", None),
        P(),
        P("seq", None, None),
        P("seq", None, None),
        P("seq", None, None),
        P(("pack", "seq"), None),
        P(("pack", "seq"), None),
        P("pack"),
    )
    out_specs = (P(("pack", "seq"), None), P(("pack", "seq"), None), P(("pack", "seq"), None))
    return jax.shard_map(shards, mesh=mesh, in_specs=in_specs, out_specs=out_specs, check_vma=False)
```

time: 584 us -> 173 us (0.30)
  the two profiles are of different devices: /device:TPU:1 before, /device:TPU:30 now
where the time goes in v1:
time: 173 us; the launch traced here: 172 us
  Pallas kernels  161 us (93%)
  local copies, waits for them, and re-layouts  10.9 us (6%)
    pallas_call x1, Pallas kernels, shards(): pl.pallas_call(functools.partial(slab_kernel, chips, window), out_shape=(...  161 us
    unnamed x25, local copies, waits for them, and re-layouts  10.2 us

profile of v1, /device:TPU:30, one launch (start us, length us, event | category | flops | bytes accessed | tf_op | source)
XLA Modules:
  0.0 172.2 jit_solution(40527358072444654)
XLA Ops:
  0.6 0.0 copy-start.9
  0.6 0.0 copy-start.5
  0.7 0.7 reshape.9.gain_ref
  1.4 0.0 copy-done.9
  1.4 0.1 copy.15.ids_ref
  1.5 0.0 copy-start.8
  1.5 0.8 copy.16.gw_ref
  2.3 0.0 copy-done.5
  2.3 0.0 copy-done.8
  2.3 0.0 copy-start
  2.3 1.1 copy-done
  3.4 0.0 copy-start.1
  3.4 1.1 copy-done.1
  4.6 0.0 copy-start.2
  4.6 1.1 copy-done.2
  5.7 1.0 copy-done.3
  6.7 0.0 copy-start.4
  6.7 0.9 copy-done.4
  7.7 0.8 copy-done.6
  8.5 0.8 copy-done.7
  9.4 160.6 %shard_map.139 = (bf16[128,2048]{1,0:T(8,128)(2,1)S(1)}, bf16[128,1024]{1,0:T(8,128)(2,1)S(1)}, bf16[128,1024]{1,0:T(8,128)(2,1)S(1)}) custom-call(s32[32]{0:T(128)S(1)} %copy-done.8, bf16[128,2048]{1,0:T(8,128)(2,1)S(1)} %copy-done.3, bf16[128,256]{1,0:T(8,128)(2,1)S(1)} %copy-done.6, bf16[128,256]{1,0:T(8,128)(2,1)S(1)} %copy-done.7, ...), custom_call_target="tpu_custom_call" | custom-call | tf_op jit(solution)/shard_map/pallas_call | solution.py:543
  169.9 0.8 copy.20
  170.7 0.7 copy.21
  171.4 0.7 copy.22
  (3 shorter events, 0.0 us)
Async XLA Ops:
  0.6 0.7 copy-start.9
  0.6 1.6 copy-start.5
  1.5 0.8 copy-start.8
  2.3 1.1 copy-start
  3.4 1.1 copy-start.1
  4.6 1.1 copy-start.2
  5.7 1.0 copy-start.3
  6.7 0.9 copy-start.4
  7.7 0.8 copy-start.6
  8.5 0.8 copy-start.7

commit v2 on v1

v2 whole, which is shorter than its diff:
```python
import functools
import math

import jax
import jax.numpy as jnp
from jax import lax
from jax.experimental import pallas as pl
from jax.experimental.pallas import tpu as pltpu
from jax.sharding import PartitionSpec as P

QUERY_HEADS = 16
KEY_VALUE_HEADS = 2
HEAD_SIZE = 128
TOP = 8
MESH = pl.DeviceIdType.MESH
HIDE = -1e30


def slab_kernel(
    chips,
    side,
    window,
    doc_ref,
    q_hbm,
    k_hbm,
    v_hbm,
    res_hbm,
    wo_hbm,
    gain_ref,
    ids_hbm,
    gw_hbm,
    wg_hbm,
    wu_hbm,
    wd_hbm,
    attn_out,
    hid_out,
    mix_out,
    kv,
    qs,
    run_max,
    run_sum,
    oacc,
    heads,
    wfull,
    res_in,
    ids_in,
    gw_in,
    hidden,
    gate_send,
    gates,
    gate_cols,
    wgu,
    wd,
    far_gu,
    far_d,
    relay_gu,
    relay_d,
    xown,
    xbuf,
    accbuf,
    home,
    contrib,
    own_part,
    in_s,
    kv_s,
    kv_r,
    sib_s,
    sib_r,
    first_s,
    first_r,
    z_s,
    z_r,
    p_s,
    p_r,
    f_s,
    f_r,
    wsib_s,
    wsib_r,
    g_s,
    g_r,
    load_s,
    ew_s,
    ew_r,
    leg_s,
    leg_r,
    o_s,
    o_r,
    os_s,
    os_r,
    x_s,
    x_r,
    a_s,
    a_r,
    h_s,
    h_r,
):
    me = lax.axis_index("seq")
    chip, core = me // 2, me % 2
    sib = chip * 2 + (1 - core)
    group = QUERY_HEADS // KEY_VALUE_HEADS
    tokens, width = res_hbm.shape
    half = tokens // 2
    kvw = k_hbm.shape[1]
    pack = lax.axis_index("pack")
    col_at, row_at = pack % side, pack // side
    w_rows = wo_hbm.shape[0]
    piece = width // (2 * side)
    mid = chips // 2
    ff = wg_hbm.shape[2]
    hops = window // 2
    first = window + 1
    reach = chips // 4

    def wrap(c):
        return lax.rem(c + 4 * chips, chips)

    def at(c):
        return wrap(c) * 2 + core

    nxt, prv = at(chip + 1), at(chip - 1)

    def rcopy(src, dst, ssem, rsem, dev, whole=False):
        return pltpu.make_async_remote_copy(
            src_ref=src,
            dst_ref=dst,
            send_sem=ssem,
            recv_sem=rsem,
            device_id=dev if whole else {"seq": dev},
            device_id_type=MESH,
        )

    def kv_hop(t, part):
        wide = pl.ds(part * kvw, kvw)
        return rcopy(
            kv.at[2 * t, :, wide],
            kv.at[2 * t + 2, :, wide],
            kv_s.at[t, part],
            kv_r.at[t, part],
            nxt,
        )

    def kv_share(t):
        return rcopy(
            kv.at[2 * t], kv.at[2 * (t - core) + 1], sib_s.at[t - core], sib_r.at[t - core], sib
        )

    def kv_shared(t):
        return rcopy(kv.at[2 * t + 1], kv.at[2 * t + 1], sib_s.at[t], sib_r.at[t], sib)

    def place(d, h):
        return mid - h if d == 0 else mid + h

    def wide_of(half_at, quarter):
        start = (half_at * side + lax.rem(quarter + side, side)) * piece
        return pl.ds(pl.multiple_of(start, 128), piece)

    def own_wide(half_at):
        return wide_of(half_at, col_at if half_at == 0 else row_at)

    def z_hop(d, h, half_at):
        wide = own_wide(half_at)
        return rcopy(
            wfull.at[place(d, h), core, :, wide],
            wfull.at[place(d, h + 1), core, :, wide],
            z_s.at[d, h, half_at],
            z_r.at[d, h, half_at],
            nxt if d == 0 else prv,
        )

    def pair(t, d):
        return pl.ds(mid - 2 * t if d == 0 else mid + 2 * t - 1, 2)

    def beside(q):
        step = 1 - 2 * (q % 2)
        if q < 2:
            return {"pack": row_at * side + lax.rem(col_at + step + side, side)}
        return {"pack": lax.rem(row_at + step + side, side) * side + col_at}

    def wide_from(q, distance):
        step = 1 - 2 * (q % 2)
        mine = col_at if q < 2 else row_at
        return wide_of(q // 2, mine - step * distance)

    def plane_copy(t, d, q):
        ref = wfull.at[pair(t, d), core, :, own_wide(q // 2)]
        return rcopy(ref, ref, p_s.at[t - 1, d, q], p_r.at[t - 1, d, q], beside(q), whole=True)

    def plane_arrived(t, d, q):
        ref = wfull.at[pair(t, d), core, :, wide_from(q, 1)]
        return rcopy(ref, ref, p_s.at[t - 1, d, q], p_r.at[t - 1, d, q], beside(q), whole=True)

    def far_rows(q):
        return pl.ds((q % 2) * (w_rows // 2), w_rows // 2)

    def far_copy(t, d, q):
        ref = wfull.at[pair(t, d), core, far_rows(q), wide_from(q, 1)]
        return rcopy(ref, ref, f_s.at[t - 1, d, q], f_r.at[t - 1, d, q], beside(q), whole=True)

    def far_arrived(t, d, q):
        ref = wfull.at[pair(t, d), core, far_rows(q), wide_from(q, 2)]
        return rcopy(ref, ref, f_s.at[t - 1, d, q], f_r.at[t - 1, d, q], beside(q), whole=True)

    def w_share(t, d):
        ref = wfull.at[pair(t, d), core]
        return rcopy(ref, ref, wsib_s.at[t, d], wsib_r.at[t, d], sib)

    def w_shared(t, d):
        ref = wfull.at[pair(t, d), 1 - core]
        return rcopy(ref, ref, wsib_s.at[t, d], wsib_r.at[t, d], sib)

    def own_share():
        ref = wfull.at[mid, core]
        return rcopy(ref, ref, wsib_s.at[0, 0], wsib_r.at[0, 0], sib)

    def own_shared():
        ref = wfull.at[mid, 1 - core]
        return rcopy(ref, ref, wsib_s.at[0, 0], wsib_r.at[0, 0], sib)

    def gate_copy(r):
        to = wrap(chip + reach - r)
        return rcopy(gate_send.at[to], gates.at[r], g_s.at[r], g_r.at[r], to * 2 + core)

    def first_copy(n, dev):
        return rcopy(kv.at[first], kv.at[first], first_s.at[n], first_r, dev)

    def cols(e):
        return pl.ds(pl.multiple_of(e * ff, 128), ff)

    def up_cols(e):
        return pl.ds(pl.multiple_of((2 + e) * ff, 128), ff)

    def rows(e):
        return pl.ds(pl.multiple_of(e * ff, 128), ff)

    weights = (
        (wg_hbm.at[0], wgu.at[:, cols(core)], wgu.at[:, cols(1 - core)]),
        (wu_hbm.at[0], wgu.at[:, up_cols(core)], wgu.at[:, up_cols(1 - core)]),
        (wd_hbm.at[0], wd.at[rows(core)], wd.at[rows(1 - core)]),
    )

    def piece_of(gu, down, n, major, minor=None, cut=None):
        if n % 2 == 0:
            count = width // side
            start = major * count
            if minor is not None:
                count = count // side
                start = start + minor * count
            if cut is not None:
                count = count // 2
                start = start + cut * count
            return gu.at[
                pl.ds(pl.multiple_of(start, 16), count), cols(core) if n == 0 else up_cols(core)
            ]
        count = ff // (2 * side)
        start = core * ff + (n // 2) * (ff // 2) + major * count
        wide, first_col = width, 0
        if minor is not None:
            wide = width // side
            first_col = minor * wide
        if cut is not None:
            wide = wide // 2
            first_col = first_col + cut * wide
        return down.at[
            pl.ds(pl.multiple_of(start, 16), count), pl.ds(pl.multiple_of(first_col, 128), wide)
        ]

    def minor_at(n):
        return col_at if n < 2 else row_at

    def major_at(n):
        return row_at if n < 2 else col_at

    def turn(at_now, by):
        return lax.rem(at_now + by + side, side)

    def leg(n, second):
        to = at(chip + reach) if n < 2 else at(chip - reach)
        held = relay_gu.at[n // 2] if n % 2 == 0 else relay_d.at[n // 2]
        if second:
            dst = piece_of(far_gu, far_d, n, major_at(n), minor_at(n))
            return rcopy(held, dst, leg_s.at[1, n], leg_r.at[1, n], to)
        src = piece_of(wgu, wd, n, major_at(n), minor_at(n))
        return rcopy(src, held, leg_s.at[0, n], leg_r.at[0, n], to)

    def opposite(stage, n, b, came=False):
        step = 1 - 2 * b
        over_x = (n < 2) == (stage < 2)
        q = b if over_x else 2 + b
        back = (stage % 2 + came) * -step
        cut = b if stage % 2 else None
        if stage < 2:
            ref = piece_of(far_gu, far_d, n, major_at(n), turn(minor_at(n), back), cut)
        else:
            ref = piece_of(far_gu, far_d, n, turn(major_at(n), back), None, cut)
        return rcopy(ref, ref, o_s.at[stage, n, b], o_r.at[stage, n, b], beside(q), whole=True)

    def opposite_step(stage):
        for n in range(4):
            if stage == 0:
                leg(n, True).wait_recv()
            if stage == 2:
                for b in range(2):
                    opposite(1, n, b, True).wait_recv()
            for b in range(2):
                if stage % 2:
                    opposite(stage - 1, n, b, True).wait_recv()
                opposite(stage, n, b).start()

    def opposite_share(mine):
        which = core if mine else 1 - core
        refs = (far_gu.at[:, cols(which)], far_gu.at[:, up_cols(which)], far_d.at[rows(which)])
        return [rcopy(r, r, os_s.at[n], os_r.at[n], sib) for n, r in enumerate(refs)]

    def unit(q, h):
        return 2 * (h - 1) + q if h < reach else 2 * (reach - 1)

    def far_end(d, q):
        return reach if d == q else reach - 1

    def x_hop(d, q, h):
        src = xown.at[q] if h == 0 else xbuf.at[unit(q, h), d]
        to = unit(q, h + 1)
        return rcopy(src, xbuf.at[to, d], x_s.at[to, d], x_r.at[to, d], nxt if d == 0 else prv)

    def a_hop(d, q, h):
        u = unit(q, h)
        to = prv if d == 0 else nxt
        if h == 1:
            return rcopy(accbuf.at[u, d], home.at[d, q], h_s.at[d, q], h_r.at[d, q], to)
        v = unit(q, h - 1)
        return rcopy(accbuf.at[u, d], accbuf.at[v, d], a_s.at[v, d], a_r.at[v, d], to)

    takes = [
        (k_hbm, kv.at[0, :, pl.ds(0, kvw)]),
        (v_hbm, kv.at[0, :, pl.ds(kvw, kvw)]),
        (wo_hbm, wfull.at[mid, core]),
        (ids_hbm, ids_in),
        (gw_hbm, gw_in),
    ]
    for h in range(QUERY_HEADS):
        takes.append(
            (
                q_hbm.at[:, pl.ds(h * HEAD_SIZE, HEAD_SIZE)],
                qs.at[h // group, pl.ds((h % group) * tokens, tokens)],
            )
        )
    takes.append((res_hbm, res_in))
    takes = [
        pltpu.make_async_copy(src, dst, in_s.at[n]) for n, (src, dst) in enumerate(takes)
    ]
    for take in takes:
        take.start()
    for n, (src, mine, _) in enumerate(weights):
        pltpu.make_async_copy(src, mine, load_s.at[n]).start()

    barrier = pltpu.get_barrier_semaphore()

    def greet(d, carry):
        pl.semaphore_signal(
            barrier, inc=1, device_id={"seq": at(chip + d)}, device_id_type=MESH
        )
        return carry

    lax.fori_loop(1, chips, greet, 0)
    pl.semaphore_signal(barrier, inc=1, device_id={"seq": sib}, device_id_type=MESH)
    for q in range(4):
        pl.semaphore_signal(barrier, inc=1, device_id=beside(q), device_id_type=MESH)
    for take in takes[:3]:
        take.wait()
    pl.semaphore_wait(barrier, chips + 4)

    for half_at in range(2):
        z_hop(1, 0, half_at).start()
        z_hop(0, 0, half_at).start()
    for part in range(2):
        kv_hop(0, part).start()

    @pl.when(core == 0)
    def _():
        kv_share(0).start()

    reached = tuple(range(chips - 1, 4, -2))

    @pl.when(me == 0)
    def _():
        for n, c in enumerate(reached):
            rcopy(kv.at[0], kv.at[first], first_s.at[n], first_r, 2 * c).start()

    own_share().start()

    @pl.when(chip < 4)
    def _():
        kv[first] = kv[0]

    for take in takes[3:]:
        take.wait()
    expert = lax.broadcasted_iota(jnp.int32, (2 * chips, tokens), 0)
    by_expert = jnp.zeros((2 * chips, tokens), jnp.float32)
    for n in range(TOP):
        by_expert = by_expert + jnp.where(
            expert == ids_in[n : n + 1, :], gw_in[n : n + 1, :], 0.0
        )
    for c in range(chips):
        far = (c + chips // 2) % chips
        gate_send[c] = jnp.concatenate(
            [by_expert[2 * c : 2 * c + 2], by_expert[2 * far : 2 * far + 2]], axis=0
        )
    gates[reach] = gate_send[chip]
    others = [r for r in range(2 * reach + 1) if r != reach]
    for r in others:
        gate_copy(r).start()

    run_max[...] = jnp.full_like(run_max, HIDE)
    run_sum[...] = jnp.zeros_like(run_sum)
    oacc[...] = jnp.zeros_like(oacc)
    factor = 1.0 / HEAD_SIZE**0.5

    def attend(slot, seen):
        key_at = lax.broadcasted_iota(jnp.int32, (tokens, tokens), 0)
        query_at = lax.broadcasted_iota(jnp.int32, (tokens, tokens), 1)
        bias = jnp.where(seen, 0.0, HIDE).astype(jnp.float32)
        late = (key_at > query_at) & (slot == 0)
        tile = jnp.where(late, HIDE, bias)
        tile = jnp.concatenate([tile] * group, axis=1)
        for g in range(KEY_VALUE_HEADS):
            keys = kv[slot, :, g * HEAD_SIZE : (g + 1) * HEAD_SIZE]
            values = kv[slot, :, kvw + g * HEAD_SIZE : kvw + (g + 1) * HEAD_SIZE]
            s = lax.dot_general(
                keys, qs[g], (((1,), (1,)), ((), ())), preferred_element_type=jnp.float32
            )
            s = s * factor + tile
            old = run_max[g]
            new = jnp.maximum(old, jnp.max(s, axis=0, keepdims=True))
            p = jnp.exp(s - new)
            fade = jnp.exp(old - new)
            run_max[g] = new
            run_sum[g] = run_sum[g] * fade + jnp.sum(p, axis=0, keepdims=True)
            oacc[g] = oacc[g] * fade + lax.dot_general(
                values,
                p.astype(jnp.bfloat16),
                (((0,), (0,)), ((), ())),
                preferred_element_type=jnp.float32,
            )

    own_doc = doc_ref[me]

    def seen_of(slot):
        blk = me - slot
        doc = doc_ref[jnp.maximum(blk, 0)]
        return (blk == 0) | ((blk > 0) & (doc == own_doc))

    def z_step(h):
        for d in range(2):
            for half_at in range(2):
                z_hop(d, h - 1, half_at).wait_recv()

                @pl.when(h < mid)
                def _():
                    z_hop(d, h, half_at).start()

    def each(action):
        for d in range(2):
            for q in range(4):
                action(d, q)

    def plane_step(t):
        each(lambda d, q: plane_copy(t, d, q).start())

    def far_step(t):
        def one(d, q):
            plane_arrived(t, d, q).wait_recv()
            far_copy(t, d, q).start()

        each(one)

    def share_step(t):
        each(lambda d, q: far_arrived(t, d, q).wait_recv())
        for d in range(2):
            w_share(t, d).start()

    for n, (src, mine, _) in enumerate(weights):
        pltpu.make_async_copy(src, mine, load_s.at[n]).wait()
        rcopy(mine, mine, ew_s.at[n], ew_r.at[n], sib).start()
    for n in range(4):
        leg(n, False).start()

    attend(0, me >= 0)

    def window_step(t, carry):
        z_step(2 * t - 1)
        for part in range(2):
            kv_hop(t - 1, part).wait_recv()

            @pl.when((t < hops - 1) | (core == 1))
            def _():
                kv_hop(t, part).start()

        kv_share(t).start()

        @pl.when(t > 1)
        def _():
            far_step(t - 1)

        z_step(2 * t)
        plane_step(t)

        @pl.when(t > 2)
        def _():
            share_step(t - 2)

        def both(n, inner):
            slot = 2 * t - n

            @pl.when(n == 1)
            def _():
                kv_shared(t - 1).wait_recv()

            attend(slot, seen_of(slot))
            return inner

        lax.fori_loop(0, 2, both, 0)

        @pl.when(t == 2)
        def _():
            for n in range(4):
                leg(n, False).wait_recv()
                leg(n, True).start()

        @pl.when((t == 2) & (core == 0) & (chip >= 5) & (chip % 2 == 1))
        def _():
            first_copy(0, sib).wait_recv()
            first_copy(0, at(chip - 1)).start()
            first_copy(1, sib).start()

        @pl.when((t == 3) & (core == 0) & (chip >= 4) & (chip % 2 == 0))
        def _():
            first_copy(1, sib).wait_recv()
            first_copy(1, sib).start()

        return carry

    lax.fori_loop(1, hops, window_step, 0)

    z_step(2 * hops - 1)

    @pl.when(core == 1)
    def _():
        for part in range(2):
            kv_hop(hops - 1, part).wait_recv()
        kv_share(hops).start()

    far_step(hops - 1)
    z_step(2 * hops)
    plane_step(hops)
    share_step(hops - 2)
    opposite_step(0)
    kv_shared(hops - 1).wait_recv()

    @pl.when((core == 1) & (chip >= 4))
    def _():
        first_copy(0, sib).wait_recv()

    def rest(n, carry):
        slot = window - 1 + 2 * n
        attend(slot, ((n == 0) & seen_of(window - 1)) | ((n == 1) & (me >= window)))
        return carry

    lax.fori_loop(0, 2, rest, 0)

    far_step(hops)
    share_step(hops - 1)
    opposite_step(1)

    for g in range(KEY_VALUE_HEADS):
        done = oacc[g] / run_sum[g]
        for n in range(group):
            h = g * group + n
            one = done[:, n * tokens : (n + 1) * tokens].T.astype(jnp.bfloat16)
            attn_out[:, h * HEAD_SIZE : (h + 1) * HEAD_SIZE] = one
            heads[h] = one

    own_shared().wait_recv()
    hidden[...] = res_in[...].astype(jnp.float32) + jnp.dot(
        heads[chip],
        wfull[mid].reshape(2 * w_rows, width),
        preferred_element_type=jnp.float32,
    )

    opposite_step(2)

    def project(t, d):
        at_pair = mid - 2 * t if d == 0 else mid + 2 * t - 1
        one = wrap(chip + at_pair - mid)
        left = heads[one]
        if d == 0:
            left = jnp.where(t == hops, jnp.zeros_like(left), left)
        both = jnp.concatenate([left, heads[wrap(one + 1)]], axis=1)
        hidden[...] += jnp.dot(
            both,
            wfull[pl.ds(at_pair, 2)].reshape(4 * w_rows, width),
            preferred_element_type=jnp.float32,
        )

    def project_step(t, carry):
        for d in range(2):
            w_shared(t, d).wait_recv()
            project(t, d)

        @pl.when(t == 1)
        def _():
            share_step(hops)

        return carry

    lax.fori_loop(1, hops + 1, project_step, 0)

    state = hidden[...]
    hid_out[...] = state.astype(jnp.bfloat16)
    mean_square = jnp.mean(state * state, axis=-1, keepdims=True)
    normed = (
        state * lax.rsqrt(mean_square + 1e-06) * gain_ref[...].astype(jnp.float32).reshape(1, width)
    ).astype(jnp.bfloat16)
    for q in range(2):
        xown[q] = normed[q * half : (q + 1) * half]
    for q in range(2):
        for d in range(2):
            x_hop(d, q, 0).start()
    opposite_step(3)

    for r in others:
        gate_copy(r).wait_recv()
    lane = lax.broadcasted_iota(jnp.int32, (half, 128), 1)
    stacked = jnp.concatenate(
        [gates[r] for r in range(2 * reach + 1)]
        + [jnp.zeros((128 - 4 * (2 * reach + 1), tokens), jnp.float32)],
        axis=0,
    )
    gate_cols[...] = stacked.T
    for n, (_, _, theirs) in enumerate(weights):
        rcopy(theirs, theirs, ew_s.at[n], ew_r.at[n], sib).wait_recv()

    def served(x, places, halves, far):
        gu, down = (far_gu, far_d) if far else (wgu, wd)
        both = jnp.dot(x, gu[...], preferred_element_type=jnp.float32)
        parts = []
        for e in range(2):
            gate = []
            for d in range(2):
                at_rows = pl.ds(pl.multiple_of(halves[d] * half, half), half)
                column = 4 * places[d] + 2 * far + e
                gate.append(
                    jnp.sum(
                        jnp.where(lane == column, gate_cols[at_rows, :], 0.0),
                        axis=1,
                        keepdims=True,
                    )
                )
            gate = jnp.concatenate(gate, axis=0)
            v = both[:, e * ff : (e + 1) * ff]
            u = both[:, (2 + e) * ff : (3 + e) * ff]
            parts.append((v / (1.0 + jnp.exp(-v)) * u * gate).astype(jnp.bfloat16))
        return jnp.dot(
            jnp.concatenate(parts, axis=1), down[...], preferred_element_type=jnp.float32
        )

    def own_served(far):
        return served(xown[...].reshape(tokens, width), (reach, reach), (0, 1), far)

    def unit_served(u, far):
        h = u // 2 + 1
        last = u == 2 * (reach - 1)
        halves = [jnp.where(last, d, u % 2) for d in range(2)]
        return served(xbuf[u].reshape(tokens, width), (reach - h, reach + h), halves, far)

    def take_x(h):
        for q in range(2):
            for d in range(2):
                if h <= far_end(d, q):
                    x_hop(d, q, h - 1).wait_recv()
                if h < far_end(d, q):
                    x_hop(d, q, h).start()

    def natural(u, carry):
        contrib[u] = unit_served(u, 0)
        return carry

    def opposed(u, carry):
        contrib[u] += unit_served(u, 1)
        return carry

    def send_sum(d, q, h):
        u = unit(q, h)
        part = contrib[u, d * half : (d + 1) * half]
        if h < far_end(d, q):
            a_hop(d, q, h + 1).wait_recv()
            part = part + accbuf[u, d].astype(jnp.float32)
        accbuf[u, d] = part.astype(jnp.bfloat16)
        a_hop(d, q, h).start()

    own_part[...] = own_served(0)
    take_x(1)
    lax.fori_loop(0, 2, natural, 0)
    for n in range(4):
        for b in range(2):
            opposite(3, n, b, True).wait_recv()
    for copy in opposite_share(True):
        copy.start()
    take_x(2)
    lax.fori_loop(2, 4, natural, 0)
    for copy in opposite_share(False):
        copy.wait_recv()
    take_x(3)
    lax.fori_loop(4, 6, natural, 0)
    lax.fori_loop(4, 6, opposed, 0)
    send_sum(0, 1, 3)
    send_sum(1, 0, 3)
    take_x(4)
    lax.fori_loop(6, 7, natural, 0)
    lax.fori_loop(6, 7, opposed, 0)
    send_sum(0, 0, 4)
    send_sum(1, 1, 4)
    lax.fori_loop(2, 4, opposed, 0)
    send_sum(0, 1, 2)
    send_sum(1, 0, 2)
    send_sum(0, 0, 3)
    send_sum(1, 1, 3)
    lax.fori_loop(0, 2, opposed, 0)
    send_sum(0, 1, 1)
    send_sum(1, 0, 1)
    send_sum(0, 0, 2)
    send_sum(1, 1, 2)
    own_part[...] += own_served(1)
    send_sum(0, 0, 1)
    send_sum(1, 1, 1)
    for q in range(2):
        part = slice(q * half, (q + 1) * half)
        total = own_part[part]
        for d in (1 - q, q):
            a_hop(d, q, 1).wait_recv()
            total = total + home[d, q].astype(jnp.float32)
        mix_out[part] = total.astype(jnp.bfloat16)

    for part in range(2):
        for t in range(hops - 1):
            kv_hop(t, part).wait_send()

        @pl.when(core == 1)
        def _():
            kv_hop(hops - 1, part).wait_send()

    for t in range(hops):
        kv_shared(t).wait_send()

    @pl.when(me == 0)
    def _():
        for n in range(len(reached)):
            first_copy(n, sib).wait_send()

    @pl.when((core == 0) & (chip >= 4))
    def _():
        first_copy(1, sib).wait_send()

    @pl.when((core == 0) & (chip >= 5) & (chip % 2 == 1))
    def _():
        first_copy(0, sib).wait_send()

    def sent_z(h, carry):
        for d in range(2):
            for half_at in range(2):
                z_hop(d, h, half_at).wait_send()
        return carry

    lax.fori_loop(0, mid, sent_z, 0)

    def sent_plane(t, carry):
        each(lambda d, q: plane_copy(t, d, q).wait_send())
        each(lambda d, q: far_copy(t, d, q).wait_send())
        for d in range(2):
            w_share(t, d).wait_send()
        return carry

    lax.fori_loop(1, hops + 1, sent_plane, 0)
    own_share().wait_send()

    for r in others:
        gate_copy(r).wait_send()
    for n in range(4):
        for second in (False, True):
            leg(n, second).wait_send()
        for stage in range(4):
            for b in range(2):
                opposite(stage, n, b).wait_send()
    for copy in opposite_share(True):
        copy.wait_send()
    for q in range(2):
        for d in range(2):
            for h in range(far_end(d, q)):
                x_hop(d, q, h).wait_send()
                a_hop(d, q, h + 1).wait_send()
    for n, (_, mine, _) in enumerate(weights):
        rcopy(mine, mine, ew_s.at[n], ew_r.at[n], sib).wait_send()


def shards(
    queries,
    token_key_heads,
    token_value_heads,
    residual,
    out_weight,
    norm_gain,
    w_gate,
    w_up,
    w_down,
    expert_ids,
    gate_weights,
    doc_of_block,
):
    blocks = lax.axis_size("seq")
    chips = blocks // 2
    tokens, width = residual.shape
    heads_width = queries.shape[1]
    kvw = token_key_heads.shape[1]
    ff = w_gate.shape[2]
    window = 8
    side = math.isqrt(lax.axis_size("pack"))
    hops = window // 2
    reach = chips // 4
    units = 2 * reach - 1
    group_rows = tokens * QUERY_HEADS // KEY_VALUE_HEADS
    half = tokens // 2
    vmem = pl.BlockSpec(memory_space=pltpu.VMEM)
    hbm = pl.BlockSpec(memory_space=pltpu.HBM)
    dma = pltpu.SemaphoreType.DMA
    bf16, f32 = jnp.bfloat16, jnp.float32
    return pl.pallas_call(
        functools.partial(slab_kernel, chips, side, window),
        out_shape=(
            jax.ShapeDtypeStruct((tokens, heads_width), bf16),
            jax.ShapeDtypeStruct((tokens, width), bf16),
            jax.ShapeDtypeStruct((tokens, width), bf16),
        ),
        in_specs=[pl.BlockSpec(memory_space=pltpu.SMEM)] + [hbm] * 5 + [vmem] + [hbm] * 5,
        out_specs=(vmem, vmem, vmem),
        scratch_shapes=[
            pltpu.VMEM((window + 2, tokens, 2 * kvw), bf16),
            pltpu.VMEM((KEY_VALUE_HEADS, group_rows, HEAD_SIZE), bf16),
            pltpu.VMEM((KEY_VALUE_HEADS, 1, group_rows), f32),
            pltpu.VMEM((KEY_VALUE_HEADS, 1, group_rows), f32),
            pltpu.VMEM((KEY_VALUE_HEADS, HEAD_SIZE, group_rows), f32),
            pltpu.VMEM((QUERY_HEADS, tokens, HEAD_SIZE), bf16),
            pltpu.VMEM((chips + 1, 2, out_weight.shape[0], width), bf16),
            pltpu.VMEM((tokens, width), bf16),
            pltpu.VMEM((TOP, tokens), jnp.int32),
            pltpu.VMEM((TOP, tokens), f32),
            pltpu.VMEM((tokens, width), f32),
            pltpu.VMEM((chips, 4, tokens), f32),
            pltpu.VMEM((2 * reach + 1, 4, tokens), f32),
            pltpu.VMEM((tokens, 128), f32),
            pltpu.VMEM((width, 4 * ff), bf16),
            pltpu.VMEM((2 * ff, width), bf16),
            pltpu.VMEM((width, 4 * ff), bf16),
            pltpu.VMEM((2 * ff, width), bf16),
            pltpu.VMEM((2, width // side**2, ff), bf16),
            pltpu.VMEM((2, ff // (2 * side), width // side), bf16),
            pltpu.VMEM((2, half, width), bf16),
            pltpu.VMEM((units, 2, half, width), bf16),
            pltpu.VMEM((units, 2, half, width), bf16),
            pltpu.VMEM((2, 2, half, width), bf16),
            pltpu.VMEM((units, tokens, width), f32),
            pltpu.VMEM((tokens, width), f32),
            dma((6 + QUERY_HEADS,)),
            dma((hops, 2)),
            dma((hops, 2)),
            dma((hops,)),
            dma((hops,)),
            dma((8,)),
            dma,
            dma((2, chips // 2, 2)),
            dma((2, chips // 2, 2)),
            dma((hops, 2, 4)),
            dma((hops, 2, 4)),
            dma((hops, 2, 4)),
            dma((hops, 2, 4)),
            dma((hops + 1, 2)),
            dma((hops + 1, 2)),
            dma((2 * reach + 1,)),
            dma((2 * reach + 1,)),
            dma((3,)),
            dma((3,)),
            dma((3,)),
            dma((2, 4)),
            dma((2, 4)),
            dma((4, 4, 2)),
            dma((4, 4, 2)),
            dma((3,)),
            dma((3,)),
            dma((units, 2)),
            dma((units, 2)),
            dma((units, 2)),
            dma((units, 2)),
            dma((2, 2)),
            dma((2, 2)),
        ],
        compiler_params=pltpu.CompilerParams(
            collective_id=0, has_side_effects=True, vmem_limit_bytes=48 << 20
        ),
    )(
        doc_of_block,
        *(pltpu.with_memory_space_constraint(a, pltpu.HBM) for a in (queries, token_key_heads, token_value_heads, residual, out_weight)),
        norm_gain,
        *(pltpu.with_memory_space_constraint(a, pltpu.HBM) for a in (expert_ids.T, gate_weights.T, w_gate, w_up, w_down)),
    )


def solution(mesh):
    in_specs = (
        P(("pack", "seq"), None),
        P(("pack", "seq"), None),
        P(("pack", "seq"), None),
        P(("pack", "seq"), None),
        P("seq", None),
        P(),
        P("seq", None, None),
        P("seq", None, None),
        P("seq", None, None),
        P(("pack", "seq"), None),
        P(("pack", "seq"), None),
        P("pack"),
    )
    out_specs = (P(("pack", "seq"), None), P(("pack", "seq"), None), P(("pack", "seq"), None))
    return jax.shard_map(shards, mesh=mesh, in_specs=in_specs, out_specs=out_specs, check_vma=False)
```

time: 173 us -> 124 us (0.72)
  the two profiles are of different devices: /device:TPU:30 before, /device:TPU:1 now
where the time goes in v2:
time: 124 us
  Pallas kernels  121 us (98%)
  local copies, waits for them, and re-layouts  2.87 us (2%)
    pallas_call x1, Pallas kernels, shards(): pl.pallas_call(functools.partial(slab_kernel, chips, side, window), out_s...  121 us
    unnamed x7, local copies, waits for them, and re-layouts  2.87 us

profile of v2, /device:TPU:1, one launch (start us, length us, event | category | flops | bytes accessed | tf_op | source)
XLA Modules:
  0.0 124.2 jit_solution(7729731739937444339)
XLA Ops:
  0.6 0.0 copy-start
  0.6 0.0 copy-start.1
  0.7 0.7 copy-done
  1.3 0.0 copy-done.1
  1.3 120.7 %shard_map.139 = (bf16[128,2048]{1,0:T(8,128)(2,1)S(1)}, bf16[128,1024]{1,0:T(8,128)(2,1)S(1)}, bf16[128,1024]{1,0:T(8,128)(2,1)S(1)}) custom-call(s32[32]{0:T(128)S(1)} %copy-done.1, bf16[128,2048]{1,0:T(8,128)(2,1)} %q_hbm.1, bf16[128,256]{1,0:T(8,128)(2,1)} %k_hbm.1, bf16[128,256]{1,0:T(8,128)(2,1)} %v_hbm.1, bf16[128,1024]{1,0:T(8,128)(2,1)} %res_hbm.1, ...), custom_call_target="tpu_custom_call" | custom-call | tf_op jit(solution)/shard_map/pallas_call | solution.py:835
  122.0 0.8 copy.18
  122.8 0.7 copy.19
  123.5 0.7 copy.20
Async XLA Ops:
  0.6 0.7 copy-start
  0.6 0.7 copy-start.1

commit v3 on v2

--- a/solution.py
+++ b/solution.py
@@ -200,6 +200,17 @@
         ref = wfull.at[pair(t, d), core, far_rows(q), wide_from(q, 2)]
         return rcopy(ref, ref, f_s.at[t - 1, d, q], f_r.at[t - 1, d, q], beside(q), whole=True)
 
+    def two_over(half_at):
+        if half_at == 0:
+            return {"pack": row_at * side + lax.rem(col_at + 2, side)}
+        return {"pack": lax.rem(row_at + 2, side) * side + col_at}
+
+    def skip_copy(d, half_at, came=False):
+        wide = wide_from(2 * half_at, 2) if came else own_wide(half_at)
+        ref = wfull.at[pair(hops, d), core, :, wide]
+        sems = f_s.at[hops - 1, d, 2 * half_at], f_r.at[hops - 1, d, 2 * half_at]
+        return rcopy(ref, ref, *sems, two_over(half_at), whole=True)
+
     def w_share(t, d):
         ref = wfull.at[pair(t, d), core]
         return rcopy(ref, ref, wsib_s.at[t, d], wsib_r.at[t, d], sib)
@@ -274,7 +285,7 @@
         return lax.rem(at_now + by + side, side)
 
     def leg(n, second):
-        to = at(chip + reach) if n < 2 else at(chip - reach)
+        to = at(chip + reach) if n % 2 else at(chip - reach)
         held = relay_gu.at[n // 2] if n % 2 == 0 else relay_d.at[n // 2]
         if second:
             dst = piece_of(far_gu, far_d, n, major_at(n), minor_at(n))
@@ -365,9 +376,11 @@
     pl.semaphore_signal(barrier, inc=1, device_id={"seq": sib}, device_id_type=MESH)
     for q in range(4):
         pl.semaphore_signal(barrier, inc=1, device_id=beside(q), device_id_type=MESH)
+    for half_at in range(2):
+        pl.semaphore_signal(barrier, inc=1, device_id=two_over(half_at), device_id_type=MESH)
     for take in takes[:3]:
         take.wait()
-    pl.semaphore_wait(barrier, chips + 4)
+    pl.semaphore_wait(barrier, chips + 6)
 
     for half_at in range(2):
         z_hop(1, 0, half_at).start()
@@ -552,6 +565,9 @@
     far_step(hops - 1)
     z_step(2 * hops)
     plane_step(hops)
+    for d in range(2):
+        for half_at in range(2):
+            skip_copy(d, half_at).start()
     share_step(hops - 2)
     opposite_step(0)
     kv_shared(hops - 1).wait_recv()
@@ -567,9 +583,12 @@
 
     lax.fori_loop(0, 2, rest, 0)
 
-    far_step(hops)
     share_step(hops - 1)
-    opposite_step(1)
+    each(lambda d, q: plane_arrived(hops, d, q).wait_recv())
+    for d in range(2):
+        for half_at in range(2):
+            skip_copy(d, half_at, True).wait_recv()
+        w_share(hops, d).start()
 
     for g in range(KEY_VALUE_HEADS):
         done = oacc[g] / run_sum[g]
@@ -586,7 +605,7 @@
         preferred_element_type=jnp.float32,
     )
 
-    opposite_step(2)
+    opposite_step(1)
 
     def project(t, d):
         at_pair = mid - 2 * t if d == 0 else mid + 2 * t - 1
@@ -605,11 +624,6 @@
         for d in range(2):
             w_shared(t, d).wait_recv()
             project(t, d)
-
-        @pl.when(t == 1)
-        def _():
-            share_step(hops)
-
         return carry
 
     lax.fori_loop(1, hops + 1, project_step, 0)
@@ -625,7 +639,7 @@
     for q in range(2):
         for d in range(2):
             x_hop(d, q, 0).start()
-    opposite_step(3)
+    opposite_step(2)
 
     for r in others:
         gate_copy(r).wait_recv()
@@ -699,18 +713,19 @@
 
     own_part[...] = own_served(0)
     take_x(1)
+    opposite_step(3)
     lax.fori_loop(0, 2, natural, 0)
+    take_x(2)
+    lax.fori_loop(2, 4, natural, 0)
     for n in range(4):
         for b in range(2):
             opposite(3, n, b, True).wait_recv()
     for copy in opposite_share(True):
         copy.start()
-    take_x(2)
-    lax.fori_loop(2, 4, natural, 0)
+    take_x(3)
+    lax.fori_loop(4, 6, natural, 0)
     for copy in opposite_share(False):
         copy.wait_recv()
-    take_x(3)
-    lax.fori_loop(4, 6, natural, 0)
     lax.fori_loop(4, 6, opposed, 0)
     send_sum(0, 1, 3)
     send_sum(1, 0, 3)
@@ -774,13 +789,20 @@
 
     def sent_plane(t, carry):
         each(lambda d, q: plane_copy(t, d, q).wait_send())
-        each(lambda d, q: far_copy(t, d, q).wait_send())
+
+        @pl.when(t < hops)
+        def _():
+            each(lambda d, q: far_copy(t, d, q).wait_send())
+
         for d in range(2):
             w_share(t, d).wait_send()
         return carry
 
     lax.fori_loop(1, hops + 1, sent_plane, 0)
     own_share().wait_send()
+    for d in range(2):
+        for half_at in range(2):
+            skip_copy(d, half_at).wait_send()
 
     for r in others:
         gate_copy(r).wait_send()

time: 124 us -> 117 us (0.944)
  Pallas kernels: 121 us -> 113 us
    pallas_call x1, Pallas kernels: 121 us -> 113 us  [shards(): pl.pallas_call(functools.partial(slab_kernel, chips, side, window), out_s...]
where the time goes in v3:
time: 117 us; the launch traced here: 116 us
  Pallas kernels  113 us (97%)
  local copies, waits for them, and re-layouts  2.87 us (2%)
    pallas_call x1, Pallas kernels, shards(): pl.pallas_call(functools.partial(slab_kernel, chips, side, window), out_s...  113 us
    unnamed x7, local copies, waits for them, and re-layouts  2.87 us

profile of v3, /device:TPU:1, one launch (start us, length us, event | category | flops | bytes accessed | tf_op | source)
XLA Modules:
  0.0 116.4 jit_solution(981555807365825513)
XLA Ops:
  0.6 0.0 copy-start
  0.6 0.0 copy-start.1
  0.7 0.7 copy-done
  1.3 0.0 copy-done.1
  1.3 112.8 %shard_map.139 = (bf16[128,2048]{1,0:T(8,128)(2,1)S(1)}, bf16[128,1024]{1,0:T(8,128)(2,1)S(1)}, bf16[128,1024]{1,0:T(8,128)(2,1)S(1)}) custom-call(s32[32]{0:T(128)S(1)} %copy-done.1, bf16[128,2048]{1,0:T(8,128)(2,1)} %q_hbm.1, bf16[128,256]{1,0:T(8,128)(2,1)} %k_hbm.1, bf16[128,256]{1,0:T(8,128)(2,1)} %v_hbm.1, bf16[128,1024]{1,0:T(8,128)(2,1)} %res_hbm.1, ...), custom_call_target="tpu_custom_call" | custom-call | tf_op jit(solution)/shard_map/pallas_call | solution.py:857
  114.2 0.8 copy.18
  115.0 0.7 copy.19
  115.7 0.7 copy.20
Async XLA Ops:
  0.6 0.7 copy-start
  0.6 0.7 copy-start.1
